TPU v7x, 512 devices: a whole 4x4x16 slice. The times are simulated.
512 devices in a mesh: gx: 32 (over z, core), vert: 16 (over y, x).
Axes of the slice: x: 4, y: 4, z: 16, core: 2. Of those that a mesh axis runs over, the one named last changes fastest.
Arguments:
- distribution: float32 [4096, 32, 256], P('vert', 'gx'), may hold values from -6 to 6
- relax_rate: float32 [32, 256], P('gx'), may hold values from 0.3 to 3
- node_weight: float32 [4096], P('vert'), may hold values from 0.05 to 1
- kernel_tiles: bfloat16 [32, 128, 1536], P('vert'), may hold values from -0.15625 to 0.15625
- tile_cols: int32 [32, 12], P('vert'), may hold values from 0 to 31, as said below
Outputs:
- new_distribution: float32 [4096, 32, 256], P('vert', 'gx')
Inputs may be any that keep to these rules, and one draw needn't show every extreme that they name: `tile_cols`: row block r lists its own block r first; the 12 column blocks listed for one row block are distinct.
All inputs are finite; a program needn't handle non-finite values.
Results may differ from a plain program's by a relative error of at most 0.0021.
Values may be sent and summed in bfloat16 or wider, within the bound.
No kernel may reach another device: no remote copies, remote signals or barrier semaphores. Data moves between devices by JAX's collectives and lax.ppermute only.
A program may use at most 64 MiB of HBM per device.

v0:
```python
import jax
import jax.numpy as jnp
from jax import lax
from jax.sharding import PartitionSpec as P

Q = 16
TILE = 128
NZ = 4
STEPS = 2
V = 4096
RBLK = 32
COURANT_SCALE = 0.3
KERNEL_STEP = 0.5
PRECISE = lax.Precision.HIGHEST


def extended(block, sides, width):
    for axis, dim in sides:
        count = lax.axis_size(axis)
        forward = [(i, i + 1) for i in range(count - 1)]
        forward.append((count - 1, 0))
        backward = [(target, source) for source, target in forward]
        low = lax.ppermute(
            lax.slice_in_dim(block, block.shape[dim] - width, None, axis=dim), axis, forward
        )
        high = lax.ppermute(lax.slice_in_dim(block, 0, width, axis=dim), axis, backward)
        block = jnp.concatenate([low, block, high], axis=dim)
    return block


def node_components(first_node, node_count):
    node_index = first_node + jnp.arange(node_count, dtype=jnp.int32)
    middle = (Q - 1) / 2.0
    speed_x = ((node_index % Q).astype(jnp.float32) - middle) / middle
    speed_y = ((node_index // Q % Q).astype(jnp.float32) - middle) / middle
    speed_z = ((node_index // (Q * Q)).astype(jnp.float32) - middle) / middle
    courant = COURANT_SCALE * jnp.stack([speed_x, speed_y, speed_z])
    squares = speed_x * speed_x + speed_y * speed_y + speed_z * speed_z
    invariants = jnp.stack([jnp.ones_like(speed_x), speed_x, speed_y, speed_z, squares])
    return (courant, invariants)


def gram_inverse(weighted, invariants):
    gram_matrix = jnp.dot(weighted, invariants.T, precision=PRECISE)
    factor = jnp.linalg.cholesky(gram_matrix)
    return jax.scipy.linalg.cho_solve((factor, True), jnp.eye(5, dtype=gram_matrix.dtype))


def advect(source, lower_x, upper_x, courant):
    plane_size = source.shape[-1]
    z_index = jnp.arange(plane_size, dtype=jnp.int32) % NZ
    lower_y = jnp.roll(source, NZ, axis=-1)
    upper_y = jnp.roll(source, -NZ, axis=-1)
    lower_z = jnp.where(
        z_index == 0, jnp.roll(source, 1 - NZ, axis=-1), jnp.roll(source, 1, axis=-1)
    )
    upper_z = jnp.where(
        z_index == NZ - 1, jnp.roll(source, NZ - 1, axis=-1), jnp.roll(source, -1, axis=-1)
    )
    total_flux = jnp.zeros_like(source)
    for component, below, above in (
        (0, lower_x, upper_x),
        (1, lower_y, upper_y),
        (2, lower_z, upper_z),
    ):
        node_speed = courant[component][:, None, None]
        total_flux = (
            total_flux
            + jnp.maximum(node_speed, 0.0) * (source - below)
            + jnp.minimum(node_speed, 0.0) * (above - source)
        )
    return source - total_flux


def apply_kernel(blocks, tile_rows, column_lists):
    cell_count = blocks.shape[-1]

    def one_block(tile_pair):
        tile_row, column_list = tile_pair
        picked = jnp.take(blocks, column_list, axis=0).reshape(-1, cell_count)
        return jnp.dot(tile_row, picked, preferred_element_type=jnp.float32)

    return lax.map(one_block, (tile_rows, column_lists))


def per_device(distribution, relax_rate, node_weight, kernel_tiles, tile_cols):
    node_local, slab_depth, plane_cells = distribution.shape
    cell_count = slab_depth * plane_cells
    first_node = lax.axis_index("vert") * node_local
    courant, invariants = node_components(first_node, node_local)
    all_weights = lax.all_gather(node_weight, "vert", axis=0, tiled=True)
    all_speeds, all_invariants = node_components(0, V)
    all_weighted = all_invariants * all_weights[None, :]
    inverse = gram_inverse(all_weighted, all_invariants)
    relax_share = relax_rate / (1.0 + relax_rate)
    current = distribution
    for step_index in range(STEPS):
        rounded = current.astype(jnp.bfloat16)
        padded = extended(current, (("gx", 1),), 1)
        lower_x = padded[:, :-2]
        upper_x = padded[:, 2:]
        advected = advect(current, lower_x, upper_x, courant)
        gathered = lax.all_gather(
            rounded.reshape(node_local, cell_count), "vert", axis=0, tiled=True
        )
        kernel_term = apply_kernel(
            gathered.reshape(RBLK, TILE, cell_count), kernel_tiles, tile_cols
        )
        explicit = advected + KERNEL_STEP * kernel_term.reshape(current.shape)
        local_weighted = invariants * node_weight[None, :]
        partial_moments = jnp.dot(
            local_weighted, explicit.reshape(node_local, cell_count), precision=PRECISE
        )
        moments = lax.psum(partial_moments, "vert")
        coeffs = jnp.dot(inverse, moments, precision=PRECISE)
        equilibrium = jnp.dot(invariants.T, coeffs, precision=PRECISE).reshape(current.shape)
        current = explicit - relax_share[None] * (explicit - equilibrium)
    return current


def solution(mesh):
    placed = (
        P("vert", "gx", None),
        P("gx", None),
        P("vert"),
        P("vert", None, None),
        P("vert", None),
    )
    return jax.shard_map(
        per_device, mesh=mesh, in_specs=placed, out_specs=P("vert", "gx", None), check_vma=False
    )
```

profile of v0, /device:TPU:32, one launch (start us, length us, event | category | flops | bytes accessed | tf_op | source)
XLA Modules:
  0.0 240.1 jit_solution(10722678696788781217)
XLA Ops:
  6.5 1.1 copy.54
  8.1 1.6 copy.68
  10.2 23.6 %all-gather.2 = f32[16,1,256]{2,1,0:T(1,128)S(1)} all-gather(f32[1,1,256]{2,1,0:T(1,128)} %bitcast.109), channel_id=1, replica_groups=mesh['gx'=32,'vert'=16] {'vert'}, dimensions={0}, use_global_device_ids=true | all-gather | bytes 17408 | tf_op jit(solution)/shard_map/all_gather | solution.py:91
  34.8 0.6 compare_reduce_fusion
  35.4 0.6 fusion.59
  36.6 0.7 add_divide_fusion
  37.7 0.7 fusion.82
  38.5 36.6 %all-gather.6.cloned.1.call-done = bf16[4096,1,256]{2,0,1:T(8,128)(2,1)} async-done(((bf16[256,1,256]{2,0,1:T(8,128)(2,1)}), bf16[4096,1,256]{2,0,1:T(8,128)(2,1)}) %all-gather.6.cloned.1.call-update) | async-done | bytes 2097168 | tf_op jit(solution)/shard_map/all_gather | solution.py:103
  75.1 5.3 %while.20 = (s32[]{:T(128)}, f32[2,128,256]{2,1,0:T(8,128)S(1)}, bf16[2,128,1536]{2,1,0:T(8,128)(2,1)S(1)}, s32[2,12]{1,0:T(2,128)S(1)}, bf16[32,128,256]{2,1,0:T(8,128)(2,1)}, /*index=5*/s32[]{:T(128)}) while((s32[]{:T(128)}, f32[2,128,256]{2,1,0:T(8,128)S(1)}, bf16[2,128,1536]{2,1,0:T(8,128)(2,1)S(1)}, s32[2,12]{1,0:T(2,128)S(1)}, ...), condition=%wide.region_1.3_spmd, body=%wide.region_0.2_spmd.sunk | while | flops 101057608 | bytes 4461865 | solution.py:83
  75.1 2.2 gather_fusion
  77.8 2.2 gather_fusion
  80.6 1.4 fusion.22
  82.3 38.7 %psum.14 = f32[5,256]{1,0:T(8,128)S(1)} all-reduce(f32[5,256]{1,0:T(8,128)S(1)} %fusion.42), channel_id=1, replica_groups=mesh['gx'=32,'vert'=16] {'vert'}, use_global_device_ids=true, to_apply=%region_4.6 | all-reduce | flops 1280 | bytes 10240 | tf_op jit(solution)/shard_map/psum | solution.py:114
  121.1 1.1 fusion.88
  122.3 0.5 collective-permute-start.2
  122.9 0.7 fusion.79
  123.6 58.2 %all-gather.8.cloned.1.call-done = bf16[4096,1,256]{0,2,1:T(8,128)(2,1)} async-done(((bf16[256,1,256]{0,2,1:T(8,128)(2,1)}), bf16[4096,1,256]{0,2,1:T(8,128)(2,1)}) %all-gather.8.cloned.1.call-update) | async-done | bytes 2097168 | tf_op jit(solution)/shard_map/all_gather | solution.py:103
  181.8 4.1 %copy.65 = bf16[4096,1,256]{2,0,1:T(8,128)(2,1)} copy(bf16[4096,1,256]{0,2,1:T(8,128)(2,1)} %all-gather.8.cloned.1.call-done) | data formatting | bytes 4194304 | tf_op jit(solution)/shard_map/while | solution.py:83
  185.9 5.3 %while.21 = (s32[]{:T(128)}, f32[2,128,256]{2,1,0:T(8,128)S(1)}, bf16[2,128,1536]{2,1,0:T(8,128)(2,1)S(1)}, s32[2,12]{1,0:T(2,128)S(1)}, bf16[32,128,256]{2,1,0:T(8,128)(2,1)}, /*index=5*/s32[]{:T(128)}) while((s32[]{:T(128)}, f32[2,128,256]{2,1,0:T(8,128)S(1)}, bf16[2,128,1536]{2,1,0:T(8,128)(2,1)S(1)}, s32[2,12]{1,0:T(2,128)S(1)}, ...), condition=%wide.region_6.8_spmd, body=%wide.region_5.7_spmd.sunk | while | flops 101057608 | bytes 4461865 | solution.py:83
  186.0 2.2 gather_fusion.1
  188.6 2.2 gather_fusion.1
  191.4 1.4 fusion.34
  193.1 38.7 %psum.15 = f32[5,256]{1,0:T(8,128)S(1)} all-reduce(f32[5,256]{1,0:T(8,128)S(1)} %fusion.40), channel_id=1, replica_groups=mesh['gx'=32,'vert'=16] {'vert'}, use_global_device_ids=true, to_apply=%region_7.9 | all-reduce | flops 1280 | bytes 10240 | tf_op jit(solution)/shard_map/psum | solution.py:114
  232.4 0.8 copy.62
  (73 shorter events, 6.2 us)
Async XLA Ops:
  6.5 68.5 %all-gather.6.cloned.1.call-start = ((), (), s32[]{:S(2)}) async-start(), calls=%async_computation | async-start | bytes 2228224 | tf_op jit(solution)/shard_map/all_gather | solution.py:103
  7.6 73.0 %collective-permute-start.1 = (f32[256,1,256]{0,2,1:T(8,128)S(1)}, f32[256,1,256]{0,2,1:T(8,128)}, u32[]{:S(2)}, u32[]{:S(2)}) collective-permute-start(f32[256,1,256]{0,2,1:T(8,128)S(1)} %copy.54), channel_id=1, source_target_pairs={{16,0},{32,16},{48,32},{64,48},{80,64},{96,80},{112,96},{128,112},... | collective-permute-start | bytes 786440 | tf_op jit(solution)/shard_map/ppermute | solution.py:26
  7.6 73.0 %collective-permute-start = (f32[256,1,256]{0,2,1:T(8,128)S(1)}, f32[256,1,256]{0,2,1:T(8,128)}, u32[]{:S(2)}, u32[]{:S(2)}) collective-permute-start(f32[256,1,256]{0,2,1:T(8,128)S(1)} %copy.54), channel_id=1, source_target_pairs={{0,16},{16,32},{32,48},{48,64},{64,80},{80,96},{96,112},{112,128},... | collective-permute-start | bytes 786440 | tf_op jit(solution)/shard_map/ppermute | solution.py:23
  9.8 65.3 %copy-start = (bf16[2,128,1536]{2,1,0:T(8,128)(2,1)S(1)}, bf16[2,128,1536]{2,1,0:T(8,128)(2,1)}, u32[]{:S(2)}) copy-start(bf16[2,128,1536]{2,1,0:T(8,128)(2,1)} %param.14) | copy-start | bytes 2359300
  9.8 65.3 %copy-start.1 = (s32[2,12]{1,0:T(2,128)S(1)}, s32[2,12]{1,0:T(2,128)}, u32[]{:S(2)}) copy-start(s32[2,12]{1,0:T(2,128)} %param.15) | copy-start | bytes 292
  9.8 172.0 %all-gather.8.cloned.1.call-start = ((), (), s32[]{:S(2)}) async-start(), calls=%async_computation.1 | async-start | bytes 2228224 | tf_op jit(solution)/shard_map/all_gather | solution.py:103
  80.4 1.6 copy-start.2
  122.2 69.2 %collective-permute-start.3 = (f32[256,1,256]{0,2,1:T(8,128)S(1)}, f32[256,1,256]{0,2,1:T(8,128)}, u32[]{:S(2)}, u32[]{:S(2)}) collective-permute-start(f32[256,1,256]{0,2,1:T(8,128)S(1)} %get-tuple-element.127), channel_id=1, source_target_pairs={{16,0},{32,16},{48,32},{64,48},{80,64},{96,80},{112,96},{128,112},... | collective-permute-start | bytes 786440 | tf_op jit(solution)/shard_map/ppermute | solution.py:26
  122.3 69.2 %collective-permute-start.2 = (f32[256,1,256]{0,2,1:T(8,128)S(1)}, f32[256,1,256]{0,2,1:T(8,128)}, u32[]{:S(2)}, u32[]{:S(2)}) collective-permute-start(f32[256,1,256]{0,2,1:T(8,128)S(1)} %get-tuple-element.127), channel_id=1, source_target_pairs={{0,16},{16,32},{32,48},{48,64},{64,80},{80,96},{96,112},{112,128},... | collective-permute-start | bytes 786440 | tf_op jit(solution)/shard_map/ppermute | solution.py:23
Sparse Core Ops, SparseCore 0:
  10.4 64.6 all-gather.5
  122.3 59.4 all-gather.7
where the time goes:
time: 241 us; the launch traced here: 240 us
  blocking collectives  101 us (42%)
  waiting for transfers between devices  94.9 us (39%)
  local copies, waits for them, and re-layouts  18.6 us (8%)
  between operations  13.7 us (6%)
  other arithmetic  6.55 us (3%)
  matrix products  4.07 us (2%)
    all_gather x2, waiting for transfers between devices, per_device(): lax.all_gather(rounded.reshape(node_local, cell_count), 'vert', axis=0, t...  94.8 us
    psum x2, blocking collectives, per_device(): moments = lax.psum(partial_moments, 'vert')  77.4 us
    all_gather x1, blocking collectives, per_device(): all_weights = lax.all_gather(node_weight, 'vert', axis=0, tiled=True)  23.6 us
    gather x4, local copies, waits for them, and re-layouts, one_block(): picked = jnp.take(blocks, column_list, axis=0).reshape(-1, cell_count)  8.75 us
  transfers between devices with their start and end apart: 6, of which 2 were waited for; matrix products, arithmetic and copies ran while one was open for 9% of the time, Pallas kernels for 0%

commit v1 on v0

--- a/solution.py
+++ b/solution.py
@@ -88,7 +88,10 @@
     cell_count = slab_depth * plane_cells
     first_node = lax.axis_index("vert") * node_local
     courant, invariants = node_components(first_node, node_local)
-    all_weights = lax.all_gather(node_weight, "vert", axis=0, tiled=True)
+    n_dev = lax.axis_size("vert")
+    tiles = jnp.stack([node_weight for _ in range(n_dev)])
+    tiles = lax.all_to_all(tiles, "vert", split_axis=0, concat_axis=0)
+    all_weights = jnp.concatenate(tiles, axis=0)
     all_speeds, all_invariants = node_components(0, V)
     all_weighted = all_invariants * all_weights[None, :]
     inverse = gram_inverse(all_weighted, all_invariants)

time: 241 us -> 251 us (1.041)
  waiting for transfers between devices: 94.9 us -> 120 us
  blocking collectives: 101 us -> 77.4 us
  starting transfers between devices: 1.07 us -> 8.15 us
    all_gather x1 -> x0, blocking collectives: 23.6 us -> none  [per_device(): all_weights = lax.all_gather(node_weight, 'vert', axis=0, tiled=True)]
    all_gather x2, waiting for transfers between devices: 94.8 us -> 116 us  [per_device(): lax.all_gather(rounded.reshape(node_local, cell_count), 'vert', axis=0, t...]
    all_to_all x0 -> x1, starting transfers between devices: none -> 7.03 us  [per_device(): tiles = lax.all_to_all(tiles, 'vert', split_axis=0, concat_axis=0)]
    all_to_all x0 -> x1, waiting for transfers between devices: none -> 3.75 us  [per_device(): tiles = lax.all_to_all(tiles, 'vert', split_axis=0, concat_axis=0)]
  transfers between devices with their start and end apart: 6 -> 7, of which waited for: 2 -> 3; matrix products, arithmetic and copies ran while one was open for 9% -> 9% of each run, Pallas kernels for 0% -> 0%
where the time goes in v1:
time: 251 us; the launch traced here: 250 us
  waiting for transfers between devices  120 us (48%)
  blocking collectives  77.4 us (31%)
  local copies, waits for them, and re-layouts  19.9 us (8%)
  between operations  13.7 us (5%)
  starting transfers between devices  8.15 us (3%)
  other arithmetic  6.53 us (3%)
  matrix products  4.09 us (2%)
    all_gather x2, waiting for transfers between devices, per_device(): lax.all_gather(rounded.reshape(node_local, cell_count), 'vert', axis=0, t...  116 us
    psum x2, blocking collectives, per_device(): moments = lax.psum(partial_moments, 'vert')  77.4 us
    gather x4, local copies, waits for them, and re-layouts, one_block(): picked = jnp.take(blocks, column_list, axis=0).reshape(-1, cell_count)  8.75 us
    all_to_all x1, starting transfers between devices, per_device(): tiles = lax.all_to_all(tiles, 'vert', split_axis=0, concat_axis=0)  7.03 us
  transfers between devices with their start and end apart: 7, of which 3 were waited for; matrix products, arithmetic and copies ran while one was open for 9% of the time, Pallas kernels for 0%

profile of v1, /device:TPU:32, one launch (start us, length us, event | category | flops | bytes accessed | tf_op | source)
XLA Modules:
  0.0 250.0 jit_solution(10390912753168074338)
XLA Ops:
  6.5 1.1 copy.54
  8.1 1.3 stack.11
  9.4 7.0 %all-to-all-start = ((f32[16,1,256]{2,1,0:T(1,128)}), f32[16,1,256]{2,1,0:T(1,128)S(1)}, u32[]{:S(2)}, u32[]{:S(2)}) async-start(f32[16,1,256]{2,1,0:T(1,128)} %stack.11), calls=%async_computation | async-start | bytes 32768 | tf_op jit(solution)/shard_map/all_to_all | solution.py:93
  16.5 1.6 copy.68
  18.3 0.7 add_divide_fusion
  19.2 0.7 fusion.82
  20.3 3.8 %all-to-all-done = f32[16,1,256]{2,1,0:T(1,128)S(1)} async-done(((f32[16,1,256]{2,1,0:T(1,128)}), f32[16,1,256]{2,1,0:T(1,128)S(1)}, u32[]{:S(2)}, u32[]{:S(2)}) %all-to-all-start) | async-done | bytes 16416 | tf_op jit(solution)/shard_map/all_to_all | solution.py:93
  25.0 0.7 compare_reduce_fusion
  27.0 58.1 %all-gather.5.cloned.1.call-done = bf16[4096,1,256]{2,0,1:T(8,128)(2,1)} async-done(((bf16[256,1,256]{2,0,1:T(8,128)(2,1)}), bf16[4096,1,256]{2,0,1:T(8,128)(2,1)}) %all-gather.5.cloned.1.call-update) | async-done | bytes 2097168 | tf_op jit(solution)/shard_map/all_gather | solution.py:106
  85.1 5.3 %while.20 = (s32[]{:T(128)}, f32[2,128,256]{2,1,0:T(8,128)S(1)}, bf16[2,128,1536]{2,1,0:T(8,128)(2,1)S(1)}, s32[2,12]{1,0:T(2,128)S(1)}, bf16[32,128,256]{2,1,0:T(8,128)(2,1)}, /*index=5*/s32[]{:T(128)}) while((s32[]{:T(128)}, f32[2,128,256]{2,1,0:T(8,128)S(1)}, bf16[2,128,1536]{2,1,0:T(8,128)(2,1)S(1)}, s32[2,12]{1,0:T(2,128)S(1)}, ...), condition=%wide.region_1.3_spmd, body=%wide.region_0.2_spmd.sunk | while | flops 101057608 | bytes 4461865 | solution.py:83
  85.1 2.2 gather_fusion
  87.8 2.2 gather_fusion
  90.6 1.4 fusion.22
  92.3 38.7 %psum.14 = f32[5,256]{1,0:T(8,128)S(1)} all-reduce(f32[5,256]{1,0:T(8,128)S(1)} %fusion.42), channel_id=1, replica_groups=mesh['gx'=32,'vert'=16] {'vert'}, use_global_device_ids=true, to_apply=%region_4.6 | all-reduce | flops 1280 | bytes 10240 | tf_op jit(solution)/shard_map/psum | solution.py:117
  131.1 1.1 fusion.88
  132.9 0.7 fusion.79
  133.6 58.2 %all-gather.7.cloned.1.call-done = bf16[4096,1,256]{0,2,1:T(8,128)(2,1)} async-done(((bf16[256,1,256]{0,2,1:T(8,128)(2,1)}), bf16[4096,1,256]{0,2,1:T(8,128)(2,1)}) %all-gather.7.cloned.1.call-update) | async-done | bytes 2097168 | tf_op jit(solution)/shard_map/all_gather | solution.py:106
  191.8 4.1 %copy.65 = bf16[4096,1,256]{2,0,1:T(8,128)(2,1)} copy(bf16[4096,1,256]{0,2,1:T(8,128)(2,1)} %all-gather.7.cloned.1.call-done) | data formatting | bytes 4194304 | tf_op jit(solution)/shard_map/while | solution.py:83
  195.9 5.3 %while.21 = (s32[]{:T(128)}, f32[2,128,256]{2,1,0:T(8,128)S(1)}, bf16[2,128,1536]{2,1,0:T(8,128)(2,1)S(1)}, s32[2,12]{1,0:T(2,128)S(1)}, bf16[32,128,256]{2,1,0:T(8,128)(2,1)}, /*index=5*/s32[]{:T(128)}) while((s32[]{:T(128)}, f32[2,128,256]{2,1,0:T(8,128)S(1)}, bf16[2,128,1536]{2,1,0:T(8,128)(2,1)S(1)}, s32[2,12]{1,0:T(2,128)S(1)}, ...), condition=%wide.region_6.8_spmd, body=%wide.region_5.7_spmd.sunk | while | flops 101057608 | bytes 4461865 | solution.py:83
  195.9 2.2 gather_fusion.1
  198.6 2.2 gather_fusion.1
  201.4 1.4 fusion.34
  203.1 38.7 %psum.15 = f32[5,256]{1,0:T(8,128)S(1)} all-reduce(f32[5,256]{1,0:T(8,128)S(1)} %fusion.40), channel_id=1, replica_groups=mesh['gx'=32,'vert'=16] {'vert'}, use_global_device_ids=true, to_apply=%region_7.9 | all-reduce | flops 1280 | bytes 10240 | tf_op jit(solution)/shard_map/psum | solution.py:117
  242.4 0.8 copy.62
  (75 shorter events, 7.3 us)
Async XLA Ops:
  7.6 83.0 %collective-permute-start.1 = (f32[256,1,256]{0,2,1:T(8,128)S(1)}, f32[256,1,256]{0,2,1:T(8,128)}, u32[]{:S(2)}, u32[]{:S(2)}) collective-permute-start(f32[256,1,256]{0,2,1:T(8,128)S(1)} %copy.54), channel_id=1, source_target_pairs={{16,0},{32,16},{48,32},{64,48},{80,64},{96,80},{112,96},{128,112},... | collective-permute-start | bytes 786440 | tf_op jit(solution)/shard_map/ppermute | solution.py:26
  7.6 83.0 %collective-permute-start = (f32[256,1,256]{0,2,1:T(8,128)S(1)}, f32[256,1,256]{0,2,1:T(8,128)}, u32[]{:S(2)}, u32[]{:S(2)}) collective-permute-start(f32[256,1,256]{0,2,1:T(8,128)S(1)} %copy.54), channel_id=1, source_target_pairs={{0,16},{16,32},{32,48},{48,64},{64,80},{80,96},{96,112},{112,128},... | collective-permute-start | bytes 786440 | tf_op jit(solution)/shard_map/ppermute | solution.py:23
  9.4 14.6 %all-to-all-start = ((f32[16,1,256]{2,1,0:T(1,128)}), f32[16,1,256]{2,1,0:T(1,128)S(1)}, u32[]{:S(2)}, u32[]{:S(2)}) async-start(f32[16,1,256]{2,1,0:T(1,128)} %stack.11), calls=%async_computation | async-start | bytes 32768 | tf_op jit(solution)/shard_map/all_to_all | solution.py:93
  16.5 68.6 %all-gather.5.cloned.1.call-start = ((), (), s32[]{:S(2)}) async-start(), calls=%async_computation.1 | async-start | bytes 2228224 | tf_op jit(solution)/shard_map/all_gather | solution.py:106
  18.2 66.9 %copy-start = (bf16[2,128,1536]{2,1,0:T(8,128)(2,1)S(1)}, bf16[2,128,1536]{2,1,0:T(8,128)(2,1)}, u32[]{:S(2)}) copy-start(bf16[2,128,1536]{2,1,0:T(8,128)(2,1)} %param.14) | copy-start | bytes 2359300
  18.2 66.9 %copy-start.1 = (s32[2,12]{1,0:T(2,128)S(1)}, s32[2,12]{1,0:T(2,128)}, u32[]{:S(2)}) copy-start(s32[2,12]{1,0:T(2,128)} %param.15) | copy-start | bytes 292
  18.2 173.6 %all-gather.7.cloned.1.call-start = ((), (), s32[]{:S(2)}) async-start(), calls=%async_computation.2 | async-start | bytes 2228224 | tf_op jit(solution)/shard_map/all_gather | solution.py:106
  90.4 1.6 copy-start.2
  132.2 69.2 %collective-permute-start.3 = (f32[256,1,256]{0,2,1:T(8,128)S(1)}, f32[256,1,256]{0,2,1:T(8,128)}, u32[]{:S(2)}, u32[]{:S(2)}) collective-permute-start(f32[256,1,256]{0,2,1:T(8,128)S(1)} %get-tuple-element.127), channel_id=1, source_target_pairs={{16,0},{32,16},{48,32},{64,48},{80,64},{96,80},{112,96},{128,112},... | collective-permute-start | bytes 786440 | tf_op jit(solution)/shard_map/ppermute | solution.py:26
  132.2 69.2 %collective-permute-start.2 = (f32[256,1,256]{0,2,1:T(8,128)S(1)}, f32[256,1,256]{0,2,1:T(8,128)}, u32[]{:S(2)}, u32[]{:S(2)}) collective-permute-start(f32[256,1,256]{0,2,1:T(8,128)S(1)} %get-tuple-element.127), channel_id=1, source_target_pairs={{0,16},{16,32},{32,48},{48,64},{64,80},{80,96},{96,112},{112,128},... | collective-permute-start | bytes 786440 | tf_op jit(solution)/shard_map/ppermute | solution.py:23
Sparse Core Ops, SparseCore 0:
  20.3 64.6 all-gather.4
  132.3 59.4 all-gather.6
